TPU v7x, 256 devices: a whole 4x4x8 slice. The times are simulated.
256 devices in a mesh: dp: 4 (over x), row: 8 (over z_lo, core), col: 8 (over z_hi, y).
Axes of the slice: x: 4, y: 4, z: 8 (z_hi: 2, z_lo: 4; z = z_hi * 4 + z_lo), core: 2. Of those that a mesh axis runs over, the one named last changes fastest.
Arguments:
- tokens: bfloat16 [4096, 8192], P(('dp', 'col'), 'row'), may hold values from -6 to 6
- gate_weight: bfloat16 [8192, 14336], P('row', ('dp', 'col')), may hold values from -0.0625 to 0.0625
- up_weight: bfloat16 [8192, 14336], P('row', ('dp', 'col')), may hold values from -0.0625 to 0.0625
- down_weight: bfloat16 [14336, 8192], P(('dp', 'col'), 'row'), may hold values from -0.046875 to 0.046875
Outputs:
- mixed: bfloat16 [4096, 8192], P(('dp', 'col'), 'row')
All inputs are finite; a program needn't handle non-finite values.
Results may differ from a plain program's by a relative error of at most 0.03.
Values may be sent and summed in bfloat16 or wider, within the bound.
A program may use at most 64 MiB of HBM per device.

v0:
```python
import jax
import jax.numpy as jnp
from jax import lax
from jax.sharding import PartitionSpec as P


def on_device(tokens, gate_weight, up_weight, down_weight):
    group_tokens = lax.all_gather(tokens, "col", axis=0, tiled=True)
    gate_cols, up_cols = (
        lax.all_gather(gate_weight, "dp", axis=1, tiled=True),
        lax.all_gather(up_weight, "dp", axis=1, tiled=True),
    )
    gate_term = jnp.dot(group_tokens, gate_cols, preferred_element_type=jnp.float32)
    up_term = jnp.dot(group_tokens, up_cols, preferred_element_type=jnp.float32)
    row_sums = lax.psum_scatter(
        jnp.concatenate((gate_term, up_term), axis=1).astype(jnp.bfloat16),
        "row",
        scatter_dimension=0,
        tiled=True,
    ).astype(jnp.float32)
    half_width = gate_cols.shape[1]
    gate_sum = row_sums[:, :half_width]
    up_sum = row_sums[:, half_width:]
    hidden = (jax.nn.silu(gate_sum) * up_sum).astype(jnp.bfloat16)
    hidden_all = lax.all_gather(hidden, "row", axis=0, tiled=True)
    down_term = jnp.dot(
        hidden_all,
        lax.all_gather(down_weight, "dp", axis=0, tiled=True),
        preferred_element_type=jnp.float32,
    )
    mixed = lax.psum_scatter(down_term.astype(jnp.bfloat16), "col", scatter_dimension=0, tiled=True)
    return mixed


def solution(mesh):
    return jax.shard_map(
        on_device,
        mesh=mesh,
        in_specs=(
            P(("dp", "col"), "row"),
            P("row", ("dp", "col")),
            P("row", ("dp", "col")),
            P(("dp", "col"), "row"),
        ),
        out_specs=P(("dp", "col"), "row"),
        check_vma=False,
    )
```

profile of v0, /device:TPU:2, one launch (start us, length us, event | category | flops | bytes accessed | tf_op | source)
XLA Modules:
  0.0 489.1 jit_solution(3508342044773073556)
XLA Ops:
  6.5 0.7 all-gather.6.cloned.1.call-update
  7.3 0.0 all-gather.8.cloned.1.call-start
  7.3 0.7 all-gather.8.cloned.1.call-update
  8.0 0.0 all-gather.10.cloned.1.call-start
  8.1 0.7 all-gather.10.cloned.1.call-update
  8.7 0.0 reduce-scatter.3.cloned.1.call-start
  8.8 80.1 %all-gather.6.cloned.1.call-done = bf16[1024,1024]{1,0:T(8,128)(2,1)} async-done(((bf16[128,1024]{1,0:T(8,128)(2,1)}), bf16[1024,1024]{1,0:T(8,128)(2,1)}) %all-gather.6.cloned.1.call-update) | async-done | bytes 2097168 | tf_op jit(solution)/shard_map/all_gather | solution.py:8
  88.9 43.2 %all-gather.8.cloned.1.call-done = bf16[1024,1792]{0,1:T(8,128)(2,1)} async-done(((bf16[1024,448]{0,1:T(8,128)(2,1)}), bf16[1024,1792]{0,1:T(8,128)(2,1)}) %all-gather.8.cloned.1.call-update) | async-done | bytes 3670032 | tf_op jit(solution)/shard_map/all_gather | solution.py:10
  132.1 8.5 %convolution_convert_fusion.1 = bf16[1024,1792]{1,0:T(8,128)(2,1)} fusion(bf16[1024,1024]{1,0:T(8,128)(2,1)} %all-gather.6.cloned.1.call-done, bf16[1024,1792]{0,1:T(8,128)(2,1)} %all-gather.8.cloned.1.call-done), kind=kOutput, calls=%fused_computation.2 | convolution fusion | flops 3759931392 | bytes 9437184 | tf_op jit(solution)/shard_map/dot_general | solution.py:13
  140.6 40.0 %all-gather.10.cloned.1.call-done = bf16[1024,1792]{0,1:T(8,128)(2,1)} async-done(((bf16[1024,448]{0,1:T(8,128)(2,1)}), bf16[1024,1792]{0,1:T(8,128)(2,1)}) %all-gather.10.cloned.1.call-update) | async-done | bytes 3670032 | tf_op jit(solution)/shard_map/all_gather | solution.py:11
  180.6 8.7 %convolution_convert_fusion = bf16[1024,1792]{1,0:T(8,128)(2,1)} fusion(bf16[1024,1024]{1,0:T(8,128)(2,1)} %all-gather.6.cloned.1.call-done, bf16[1024,1792]{0,1:T(8,128)(2,1)} %all-gather.10.cloned.1.call-done), kind=kOutput, calls=%fused_computation.1 | convolution fusion | flops 3759931392 | bytes 9437184 | tf_op jit(solution)/shard_map/dot_general | solution.py:14
  189.3 5.5 %pad_maximum_fusion = bf16[1024,3584]{1,0:T(8,128)(2,1)} fusion(bf16[1024,1792]{1,0:T(8,128)(2,1)} %convolution_convert_fusion, bf16[1024,1792]{1,0:T(8,128)(2,1)S(1)} %copy-done), kind=kLoop, calls=%fused_computation | loop fusion | flops 14680064 | bytes 14680064 | tf_op jit(solution)/shard_map/concatenate | solution.py:16
  194.8 0.0 reduce-scatter.3.cloned.1.call-update
  194.9 0.0 all-gather.14.cloned.1.call-start
  194.9 0.5 all-gather.14.cloned.1.call-update
  195.5 0.0 all-gather.12.cloned.1.call-start
  195.5 85.4 %reduce-scatter.3.cloned.1.call-done = bf16[128,3584]{1,0:T(8,128)(2,1)} async-done(((bf16[1024,3584]{1,0:T(8,128)(2,1)}), bf16[128,3584]{1,0:T(8,128)(2,1)}) %reduce-scatter.3.cloned.1.call-update) | async-done | bytes 917520 | tf_op jit(solution)/shard_map/reduce_scatter | solution.py:15
  280.9 1.4 convert_element_type.10
  282.3 1.0 fusion
  283.3 0.0 reduce-scatter.5.cloned.1.call-start
  283.4 43.5 %all-gather.14.cloned.1.call-done = bf16[1792,1024]{1,0:T(8,128)(2,1)} async-done(((bf16[448,1024]{1,0:T(8,128)(2,1)}), bf16[1792,1024]{1,0:T(8,128)(2,1)}) %all-gather.14.cloned.1.call-update) | async-done | bytes 3670032 | tf_op jit(solution)/shard_map/all_gather | solution.py:28
  326.9 52.3 %all-gather.12.cloned.1.call-done = bf16[1024,1792]{1,0:T(8,128)(2,1)} async-done(((bf16[128,1792]{1,0:T(8,128)(2,1)}), bf16[1024,1792]{1,0:T(8,128)(2,1)}) %all-gather.12.cloned.1.call-update) | async-done | bytes 3670032 | tf_op jit(solution)/shard_map/all_gather | solution.py:25
  379.2 8.4 %convolution_convert_fusion.2 = bf16[1024,1024]{1,0:T(8,128)(2,1)} fusion(bf16[1024,1792]{1,0:T(8,128)(2,1)} %all-gather.12.cloned.1.call-done, bf16[1792,1024]{1,0:T(8,128)(2,1)} %all-gather.14.cloned.1.call-done), kind=kOutput, calls=%fused_computation.3 | convolution fusion | flops 3759144960 | bytes 9437184 | tf_op jit(solution)/shard_map/dot_general | solution.py:26
  387.6 94.6 %reduce-scatter.5.cloned.1.call-done = bf16[128,1024]{1,0:T(8,128)(2,1)} async-done(((bf16[1024,1024]{1,0:T(8,128)(2,1)}), bf16[128,1024]{1,0:T(8,128)(2,1)}) %reduce-scatter.5.cloned.1.call-update) | async-done | bytes 262160 | tf_op jit(solution)/shard_map/reduce_scatter | solution.py:31
  (5 shorter events, 0.0 us)
Async XLA Ops:
  6.5 82.4 %all-gather.6.cloned.1.call-start = ((), (), s32[]{:S(2)}) async-start(), calls=%async_computation.2 | async-start | bytes 2359296 | tf_op jit(solution)/shard_map/all_gather | solution.py:8
  7.3 124.9 %all-gather.8.cloned.1.call-start = ((), (), s32[]{:S(2)}) async-start(), calls=%async_computation.3 | async-start | bytes 4587520 | tf_op jit(solution)/shard_map/all_gather | solution.py:10
  8.0 172.6 %all-gather.10.cloned.1.call-start = ((), (), s32[]{:S(2)}) async-start(), calls=%async_computation.4 | async-start | bytes 4587520 | tf_op jit(solution)/shard_map/all_gather | solution.py:11
  8.7 272.2 %reduce-scatter.3.cloned.1.call-start = ((), (), s32[]{:S(2)}) async-start(), calls=%async_computation.5 | async-start | bytes 8257536 | tf_op jit(solution)/shard_map/reduce_scatter | solution.py:15
  180.6 8.7 %copy-start = (bf16[1024,1792]{1,0:T(8,128)(2,1)S(1)}, bf16[1024,1792]{1,0:T(8,128)(2,1)}, u32[]{:S(2)}) copy-start(bf16[1024,1792]{1,0:T(8,128)(2,1)} %convolution_convert_fusion.1) | copy-start | bytes 11010052
  194.9 132.0 %all-gather.14.cloned.1.call-start = ((), (), s32[]{:S(2)}) async-start(), calls=%async_computation.7 | async-start | bytes 4587520 | tf_op jit(solution)/shard_map/all_gather | solution.py:28
  195.5 183.7 %all-gather.12.cloned.1.call-start = ((), (), s32[]{:S(2)}) async-start(), calls=%async_computation.6 | async-start | bytes 4128768 | tf_op jit(solution)/shard_map/all_gather | solution.py:25
  283.3 198.9 %reduce-scatter.5.cloned.1.call-start = ((), (), s32[]{:S(2)}) async-start(), calls=%async_computation.8 | async-start | bytes 2359296 | tf_op jit(solution)/shard_map/reduce_scatter | solution.py:31
Sparse Core Ops, SparseCore 0:
  10.0 78.8 all-gather.5
  90.7 41.3 all-gather.7
  133.9 46.6 all-gather.9
  195.0 85.8 reduce-scatter.2
  282.6 44.2 all-gather.13
  328.5 50.5 all-gather.11
  387.7 94.4 reduce-scatter.4
where the time goes:
time: 489 us
  waiting for transfers between devices  442 us (90%)
  matrix products  25.7 us (5%)
  between operations  13.5 us (3%)
  other arithmetic  7.89 us (2%)
    reduce_scatter x1, waiting for transfers between devices, on_device(): lax.psum_scatter(down_term.astype(jnp.bfloat16), 'col', scatter_dimension...  94.6 us
    reduce_scatter x1, waiting for transfers between devices, on_device(): lax.psum_scatter(jnp.concatenate((gate_term, up_term), axis=1).astype(jnp...  85.4 us
    all_gather x1, waiting for transfers between devices, on_device(): group_tokens = lax.all_gather(tokens, 'col', axis=0, tiled=True)  80.1 us
    all_gather x1, waiting for transfers between devices, on_device(): hidden_all = lax.all_gather(hidden, 'row', axis=0, tiled=True)  52.3 us
    all_gather x1, waiting for transfers between devices, on_device(): lax.all_gather(down_weight, 'dp', axis=0, tiled=True)  43.5 us
    all_gather x1, waiting for transfers between devices, on_device(): lax.all_gather(gate_weight, 'dp', axis=1, tiled=True)  43.2 us
    all_gather x1, waiting for transfers between devices, on_device(): lax.all_gather(up_weight, 'dp', axis=1, tiled=True)  40 us
  transfers between devices with their start and end apart: 7, of which 7 were waited for; matrix products, arithmetic and copies ran while one was open for 2% of the time, Pallas kernels for 0%

commit v1 on v0

--- a/solution.py
+++ b/solution.py
@@ -1,13 +1,45 @@
+import functools
 import jax
 import jax.numpy as jnp
 from jax import lax
 from jax.sharding import PartitionSpec as P
 
 
+def expand_terms(state, ax_name, k_dim):
+    far_arr, raw_out, y2 = (lax.psum(1, ax_name), lax.axis_index(ax_name), state.shape[k_dim])
+    fields = []
+    for h, j in enumerate(state.shape):
+        fields.append(j * far_arr if h == k_dim else j)
+    mixed_arr = lax.dynamic_update_slice_in_dim(
+        jnp.zeros(fields, state.dtype), state, raw_out * y2, axis=k_dim
+    )
+    work_now = lower = state
+    for w in range(1, far_arr // 2 + 1):
+        block_list = []
+        for h in range(far_arr):
+            block_list.append((h, (h + 1) % far_arr))
+        work_now = lax.ppermute(work_now, ax_name, block_list)
+        mixed_arr = lax.dynamic_update_slice_in_dim(
+            mixed_arr, work_now, (raw_out - w) % far_arr * y2, axis=k_dim
+        )
+        if 2 * w < far_arr:
+            tray = []
+            for h in range(far_arr):
+                tray.append((h, (h - 1) % far_arr))
+            lower = lax.ppermute(lower, ax_name, tray)
+            mixed_arr = lax.dynamic_update_slice_in_dim(
+                mixed_arr, lower, (raw_out + w) % far_arr * y2, axis=k_dim
+            )
+    return mixed_arr
+
+
+edit_rows = functools.partial(expand_terms, ax_name="dp", k_dim=1)
+
+
 def on_device(tokens, gate_weight, up_weight, down_weight):
     group_tokens = lax.all_gather(tokens, "col", axis=0, tiled=True)
     gate_cols, up_cols = (
-        lax.all_gather(gate_weight, "dp", axis=1, tiled=True),
+        edit_rows(gate_weight),
         lax.all_gather(up_weight, "dp", axis=1, tiled=True),
     )
     gate_term = jnp.dot(group_tokens, gate_cols, preferred_element_type=jnp.float32)

time: 489 us -> 452 us (0.924)
  waiting for transfers between devices: 442 us -> 382 us
  local copies, waits for them, and re-layouts: 0.01 us -> 19.1 us
    reduce_scatter x1 -> x0, waiting for transfers between devices: 85.4 us -> none  [on_device(): lax.psum_scatter(jnp.concatenate((gate_term, up_term), axis=1).astype(jnp...]
    unnamed x7, waiting for transfers between devices: 2.67 us -> 87.2 us
    all_gather x1, waiting for transfers between devices: 80.1 us -> 36.4 us  [on_device(): group_tokens = lax.all_gather(tokens, 'col', axis=0, tiled=True)]
    all_gather x1 -> x0, waiting for transfers between devices: 43.2 us -> none  [on_device(): lax.all_gather(gate_weight, 'dp', axis=1, tiled=True)]
    ppermute x0 -> x3, waiting for transfers between devices: none -> 33 us  [the longest x2 33 us: expand_terms(): work_now = lax.ppermute(work_now, ax_name, block_list)]
    unnamed x2 -> x6, local copies, waits for them, and re-layouts: 0.01 us -> 11.5 us
    all_gather x1, waiting for transfers between devices: 40 us -> 34.6 us  [on_device(): lax.all_gather(up_weight, 'dp', axis=1, tiled=True)]
    dynamic_update_slice x0 -> x4, local copies, waits for them, and re-layouts: none -> 5.22 us  [the longest x1 2.18 us: expand_terms(): lax.dynamic_update_slice_in_dim(mixed_arr, lower, (raw_out + w) % far_arr...]
  transfers between devices with their start and end apart: 7 -> 9, of which waited for: 7 -> 8; matrix products, arithmetic and copies ran while one was open for 2% -> 4% of each run, Pallas kernels for 0% -> 0%
where the time goes in v1:
time: 452 us; the launch traced here: 451 us
  waiting for transfers between devices  382 us (85%)
  matrix products  25.8 us (6%)
  local copies, waits for them, and re-layouts  19.1 us (4%)
  between operations  13.5 us (3%)
  other arithmetic  7.03 us (2%)
    reduce_scatter x1, waiting for transfers between devices, on_device(): lax.psum_scatter(down_term.astype(jnp.bfloat16), 'col', scatter_dimension...  96.4 us
    unnamed x7, waiting for transfers between devices  87.2 us
    all_gather x1, waiting for transfers between devices, on_device(): hidden_all = lax.all_gather(hidden, 'row', axis=0, tiled=True)  50.8 us
    all_gather x1, waiting for transfers between devices, on_device(): lax.all_gather(down_weight, 'dp', axis=0, tiled=True)  43.2 us
    all_gather x1, waiting for transfers between devices, on_device(): group_tokens = lax.all_gather(tokens, 'col', axis=0, tiled=True)  36.4 us
    all_gather x1, waiting for transfers between devices, on_device(): lax.all_gather(up_weight, 'dp', axis=1, tiled=True)  34.6 us
    ppermute x2, waiting for transfers between devices, expand_terms(): work_now = lax.ppermute(work_now, ax_name, block_list)  33 us
    unnamed x6, local copies, waits for them, and re-layouts  11.5 us
  transfers between devices with their start and end apart: 9, of which 8 were waited for; matrix products, arithmetic and copies ran while one was open for 4% of the time, Pallas kernels for 0%

profile of v1, /device:TPU:2, one launch (start us, length us, event | category | flops | bytes accessed | tf_op | source)
XLA Modules:
  0.0 451.3 jit_solution(12194176516375075834)
XLA Ops:
  6.5 0.7 all-gather.5.cloned.1.call-update
  8.1 1.6 collective-permute-start
  9.6 0.8 collective-permute-start.1
  10.5 20.0 %collective-permute-done = bf16[1024,448]{0,1:T(8,128)(2,1)S(1)} collective-permute-done((bf16[1024,448]{0,1:T(8,128)(2,1)}, bf16[1024,448]{0,1:T(8,128)(2,1)S(1)}, u32[]{:S(2)}, u32[]{:S(2)}) %collective-permute-start) | collective-permute-done | bytes 917536 | tf_op jit(solution)/shard_map/ppermute | solution.py:21
  30.4 1.5 collective-permute-start.2
  31.9 2.3 broadcast_in_dim.3
  34.2 1.0 constant_dynamic-update-slice_fusion.3
  35.3 1.0 constant_dynamic-update-slice_fusion.2
  36.3 2.2 constant_dynamic-update-slice_fusion.1
  38.5 13.1 %collective-permute-done.2 = bf16[1024,448]{0,1:T(8,128)(2,1)S(1)} collective-permute-done((bf16[1024,448]{0,1:T(8,128)(2,1)S(1)}, bf16[1024,448]{0,1:T(8,128)(2,1)S(1)}, u32[]{:S(2)}, u32[]{:S(2)}) %collective-permute-start.2) | collective-permute-done | bytes 917536 | tf_op jit(solution)/shard_map/ppermute | solution.py:21
  51.5 1.0 constant_dynamic-update-slice_fusion
  52.5 36.4 %all-gather.5.cloned.1.call-done = bf16[1024,1024]{1,0:T(8,128)(2,1)} async-done(((bf16[128,1024]{1,0:T(8,128)(2,1)}), bf16[1024,1024]{1,0:T(8,128)(2,1)}) %all-gather.5.cloned.1.call-update) | async-done | bytes 2097168 | tf_op jit(solution)/shard_map/all_gather | solution.py:40
  88.9 8.6 %fusion = bf16[1024,1792]{0,1:T(8,128)(2,1)} fusion(bf16[1024,1792]{0,1:T(8,128)(2,1)} %constant_dynamic-update-slice_fusion, bf16[1024,1024]{1,0:T(8,128)(2,1)} %all-gather.5.cloned.1.call-done), kind=kOutput, calls=%fused_computation.3 | convolution fusion | flops 3759931392 | bytes 9437184 | tf_op jit(solution)/shard_map/dot_general | solution.py:45
  97.5 34.6 %all-gather.7.cloned.1.call-done = bf16[1024,1792]{0,1:T(8,128)(2,1)} async-done(((bf16[1024,448]{0,1:T(8,128)(2,1)}), bf16[1024,1792]{0,1:T(8,128)(2,1)}) %all-gather.7.cloned.1.call-update) | async-done | bytes 3670032 | tf_op jit(solution)/shard_map/all_gather | solution.py:43
  132.1 8.7 %convolution_convert_fusion = bf16[1024,1792]{0,1:T(8,128)(2,1)} fusion(bf16[1024,1024]{1,0:T(8,128)(2,1)} %all-gather.5.cloned.1.call-done, bf16[1024,1792]{0,1:T(8,128)(2,1)} %all-gather.7.cloned.1.call-done), kind=kOutput, calls=%fused_computation.1 | convolution fusion | flops 3759931392 | bytes 9437184 | tf_op jit(solution)/shard_map/dot_general | solution.py:46
  140.8 5.9 %pad_maximum_fusion = bf16[1024,3584]{0,1:T(8,128)(2,1)} fusion(bf16[1024,1792]{0,1:T(8,128)(2,1)} %convolution_convert_fusion, bf16[1024,1792]{0,1:T(8,128)(2,1)S(1)} %copy-done), kind=kLoop, calls=%fused_computation | loop fusion | flops 14680064 | bytes 14680064 | tf_op jit(solution)/shard_map/concatenate | solution.py:48
  146.7 10.0 %copy.8 = bf16[1024,3584]{1,0:T(8,128)(2,1)} copy(bf16[1024,3584]{0,1:T(8,128)(2,1)} %pad_maximum_fusion) | data formatting | bytes 14680064
  157.5 85.2 %reduce-scatter.7.cloned.1.call-done = bf16[128,3584]{1,0:T(8,128)(2,1)} async-done(((bf16[1024,3584]{1,0:T(8,128)(2,1)}), bf16[128,3584]{1,0:T(8,128)(2,1)}) %reduce-scatter.7.cloned.1.call-update) | async-done | bytes 917520
  242.8 1.5 copy.9
  244.5 1.0 fusion.1
  245.5 43.2 %all-gather.11.cloned.1.call-done = bf16[1792,1024]{1,0:T(8,128)(2,1)} async-done(((bf16[448,1024]{1,0:T(8,128)(2,1)}), bf16[1792,1024]{1,0:T(8,128)(2,1)}) %all-gather.11.cloned.1.call-update) | async-done | bytes 3670032 | tf_op jit(solution)/shard_map/all_gather | solution.py:60
  288.7 50.8 %all-gather.9.cloned.1.call-done = bf16[1024,1792]{0,1:T(8,128)(2,1)} async-done(((bf16[128,1792]{0,1:T(8,128)(2,1)}), bf16[1024,1792]{0,1:T(8,128)(2,1)}) %all-gather.9.cloned.1.call-update) | async-done | bytes 3670032 | tf_op jit(solution)/shard_map/all_gather | solution.py:57
  339.5 8.5 %convolution_convert_fusion.2 = bf16[1024,1024]{1,0:T(8,128)(2,1)} fusion(bf16[1024,1792]{0,1:T(8,128)(2,1)} %all-gather.9.cloned.1.call-done, bf16[1792,1024]{1,0:T(8,128)(2,1)} %all-gather.11.cloned.1.call-done), kind=kOutput, calls=%fused_computation.4 | convolution fusion | flops 3759144960 | bytes 9437184 | tf_op jit(solution)/shard_map/dot_general | solution.py:58
  348.1 96.4 %reduce-scatter.5.cloned.1.call-done = bf16[128,1024]{1,0:T(8,128)(2,1)} async-done(((bf16[1024,1024]{1,0:T(8,128)(2,1)}), bf16[128,1024]{1,0:T(8,128)(2,1)}) %reduce-scatter.5.cloned.1.call-update) | async-done | bytes 262160 | tf_op jit(solution)/shard_map/reduce_scatter | solution.py:63
  (17 shorter events, 1.8 us)
Async XLA Ops:
  6.5 27.7 %copy-start.1 = (bf16[1024,448]{0,1:T(8,128)(2,1)S(1)}, bf16[1024,448]{0,1:T(8,128)(2,1)}, u32[]{:S(2)}) copy-start(bf16[1024,448]{0,1:T(8,128)(2,1)} %param.5) | copy-start | bytes 2752516
  6.5 82.4 %all-gather.5.cloned.1.call-start = ((), (), s32[]{:S(2)}) async-start(), calls=%async_computation.2 | async-start | bytes 2359296 | tf_op jit(solution)/shard_map/all_gather | solution.py:40
  7.3 124.9 %all-gather.7.cloned.1.call-start = ((), (), s32[]{:S(2)}) async-start(), calls=%async_computation.3 | async-start | bytes 4587520 | tf_op jit(solution)/shard_map/all_gather | solution.py:43
  8.0 234.8 %reduce-scatter.7.cloned.1.call-start = ((), (), s32[]{:S(2)}) async-start(), calls=%async_computation.7 | async-start | bytes 8257536
  8.1 22.4 %collective-permute-start = (bf16[1024,448]{0,1:T(8,128)(2,1)}, bf16[1024,448]{0,1:T(8,128)(2,1)S(1)}, u32[]{:S(2)}, u32[]{:S(2)}) collective-permute-start(bf16[1024,448]{0,1:T(8,128)(2,1)} %param.5), channel_id=1, source_target_pairs={{0,64},{64,128},{128,192},{192,0},{1,65},{65,129},{129,193},{193,1... | collective-permute-start | bytes 2752520 | tf_op jit(solution)/shard_map/ppermute | solution.py:21
  9.6 26.7 %collective-permute-start.1 = (bf16[1024,448]{0,1:T(8,128)(2,1)}, bf16[1024,448]{0,1:T(8,128)(2,1)}, u32[]{:S(2)}, u32[]{:S(2)}) collective-permute-start(bf16[1024,448]{0,1:T(8,128)(2,1)} %param.5), channel_id=1, source_target_pairs={{0,192},{64,0},{128,64},{192,128},{1,193},{65,1},{129,65},{193,129... | collective-permute-start | bytes 2752520 | tf_op jit(solution)/shard_map/ppermute | solution.py:29
  30.4 21.1 %collective-permute-start.2 = (bf16[1024,448]{0,1:T(8,128)(2,1)S(1)}, bf16[1024,448]{0,1:T(8,128)(2,1)S(1)}, u32[]{:S(2)}, u32[]{:S(2)}) collective-permute-start(bf16[1024,448]{0,1:T(8,128)(2,1)S(1)} %collective-permute-done), channel_id=1, source_target_pairs={{0,64},{64,128},{128,192},{192,0},{1,65},{65,129},{129,193},{193,1... | collective-permute-start | bytes 2752520 | tf_op jit(solution)/shard_map/ppermute | solution.py:21
  132.1 8.7 %copy-start = (bf16[1024,1792]{0,1:T(8,128)(2,1)S(1)}, bf16[1024,1792]{0,1:T(8,128)(2,1)}, u32[]{:S(2)}) copy-start(bf16[1024,1792]{0,1:T(8,128)(2,1)} %fusion) | copy-start | bytes 11010052
  156.7 132.0 %all-gather.11.cloned.1.call-start = ((), (), s32[]{:S(2)}) async-start(), calls=%async_computation.5 | async-start | bytes 4587520 | tf_op jit(solution)/shard_map/all_gather | solution.py:60
  157.3 182.2 %all-gather.9.cloned.1.call-start = ((), (), s32[]{:S(2)}) async-start(), calls=%async_computation.4 | async-start | bytes 4128768 | tf_op jit(solution)/shard_map/all_gather | solution.py:57
  245.5 199.0 %reduce-scatter.5.cloned.1.call-start = ((), (), s32[]{:S(2)}) async-start(), calls=%async_computation.6 | async-start | bytes 2359296 | tf_op jit(solution)/shard_map/reduce_scatter | solution.py:63
Sparse Core Ops, SparseCore 0:
  10.0 78.8 all-gather.4
  90.7 41.3 all-gather.6
  156.8 85.8 reduce-scatter.6
  244.4 44.2 all-gather.10
  290.3 49.1 all-gather.8
  348.2 96.2 reduce-scatter.4
